TPU v7x, 8 devices: a whole 2x2x1 slice. The times are simulated.
8 devices in a mesh: dp: 2 (over z, y), fsdp: 4 (over x, core).
Axes of the slice: x: 2, y: 2, z: 1, core: 2. Of those that a mesh axis runs over, the one named last changes fastest.
Arguments:
- u_in: bfloat16 [8, 1024, 2560], P(('dp', 'fsdp'))
- grad_out: bfloat16 [8, 1024, 2560], P(('dp', 'fsdp'))
- norm_w: bfloat16 [2, 2560], P(None, 'fsdp')
- w_in: bfloat16 [2, 2560, 10576], P(None, 'fsdp')
- conv_w: bfloat16 [2, 4, 5376], P(None, None, 'fsdp')
- conv_b: bfloat16 [2, 5376], P(None, 'fsdp')
- dt_bias: float32 [2, 80], P(None, 'fsdp')
- a_log: float32 [2, 80], P(None, 'fsdp')
- d_skip: float32 [2, 80], P(None, 'fsdp')
- gate_w: bfloat16 [2, 5120], P(None, 'fsdp')
- w_out: bfloat16 [2, 5120, 2560], P(None, 'fsdp')
Outputs:
- output 1: bfloat16 [8, 1024, 2560], P(('dp', 'fsdp'))
- output 2: bfloat16 [8, 1024, 2560], P(('dp', 'fsdp'))
- output 3: float32 [2, 2560], P(None, 'fsdp')
- output 4: float32 [2, 2560, 10576], P(None, 'fsdp')
- output 5: float32 [2, 4, 5376], P(None, None, 'fsdp')
- output 6: float32 [2, 5376], P(None, 'fsdp')
- output 7: float32 [2, 80], P(None, 'fsdp')
- output 8: float32 [2, 80], P(None, 'fsdp')
- output 9: float32 [2, 80], P(None, 'fsdp')
- output 10: float32 [2, 5120], P(None, 'fsdp')
- output 11: float32 [2, 5120, 2560], P(None, 'fsdp')
All inputs are finite; a program needn't handle non-finite values.
Results may differ from a plain program's by a relative error of at most 0.02.
Values are sent between devices in bfloat16 or wider.
A program may use at most 1 GiB of HBM per device.

v0:
```python
import jax
import jax.numpy as jnp
from jax import lax
from jax.sharding import PartitionSpec as P

CHUNK_LEN = 256
STATE_DIM = 128
NORM_EPS = 1e-5
GATHER_AXES = (0, 0, 1, 0, 0, 0, 0, 0, 0)


def pre_norm(u_rows, norm_w):
    rows_f = u_rows.astype(jnp.float32)
    inv_rms = lax.rsqrt(jnp.mean(jnp.square(rows_f), axis=-1, keepdims=True) + NORM_EPS)
    return (rows_f * inv_rms * norm_w.astype(jnp.float32)).astype(jnp.bfloat16)


def ssd_chunks(x_heads, dt_heads, a_heads, b_mat, c_mat):
    n_batch, seq_len, n_heads, head_dim = x_heads.shape
    n_groups = b_mat.shape[2]
    per_group = n_heads // n_groups
    n_chunks = seq_len // CHUNK_LEN
    block_shape = (n_batch, n_chunks, CHUNK_LEN, n_groups)
    x_dt = (x_heads * dt_heads[..., None]).reshape(block_shape + (per_group, head_dim))
    cum_a = jnp.cumsum(a_heads.reshape(block_shape + (per_group,)), axis=2)
    b_chunk = b_mat.reshape(block_shape + (STATE_DIM,))
    c_chunk = c_mat.reshape(block_shape + (STATE_DIM,))
    scores = jnp.einsum('bcqgn,bcsgn->bcgqs', c_chunk, b_chunk, preferred_element_type=jnp.float32)
    cum_t = jnp.moveaxis(cum_a, 2, -1)
    log_gap = cum_t[..., :, None] - cum_t[..., None, :]
    causal = jnp.arange(CHUNK_LEN)[:, None] >= jnp.arange(CHUNK_LEN)[None, :]
    decay_mat = jnp.where(causal, jnp.exp(jnp.where(causal, log_gap, 0.0)), 0.0)
    y_diag = jnp.einsum('bcgrqs,bcsgrp->bcqgrp', scores[:, :, :, None] * decay_mat, x_dt, preferred_element_type=jnp.float32)
    end_decay = jnp.exp(cum_a[:, :, -1:] - cum_a)
    states = jnp.einsum('bcsgn,bcsgrp->bcgrpn', b_chunk, x_dt * end_decay[..., None], preferred_element_type=jnp.float32)
    totals = cum_a[:, :, -1]
    incl_sum = jnp.cumsum(totals, axis=1)
    excl_sum = incl_sum - totals
    chunk_gap = jnp.moveaxis(excl_sum, 1, -1)[..., :, None] - jnp.moveaxis(incl_sum, 1, -1)[..., None, :]
    earlier = jnp.arange(n_chunks)[:, None] > jnp.arange(n_chunks)[None, :]
    carry_mat = jnp.where(earlier, jnp.exp(jnp.where(earlier, chunk_gap, 0.0)), 0.0)
    prev_state = jnp.einsum('bgrij,bjgrpn->bigrpn', carry_mat, states, preferred_element_type=jnp.float32)
    y_off = jnp.einsum('bcqgn,bcgrpn->bcqgrp', c_chunk, prev_state, preferred_element_type=jnp.float32) * jnp.exp(cum_a)[..., None]
    return (y_diag + y_off).reshape(x_heads.shape)


def mixer_core(proj_out, conv_w, conv_b, dt_bias, a_log, d_skip, gate_w):
    n_batch, seq_len, _ = proj_out.shape
    d_inner = gate_w.shape[0]
    conv_dim = conv_b.shape[0]
    n_heads = dt_bias.shape[0]
    n_taps = conv_w.shape[0]
    n_groups = (conv_dim - d_inner) // (2 * STATE_DIM)
    group_w = n_groups * STATE_DIM
    padded = jnp.pad(proj_out[:, :, d_inner:d_inner + conv_dim], ((0, 0), (n_taps - 1, 0), (0, 0)))
    conv_out = conv_b.astype(jnp.float32) + sum(padded[:, tap:tap + seq_len] * conv_w[tap].astype(jnp.float32) for tap in range(n_taps))
    xbc_act = jax.nn.silu(conv_out)
    x_heads = xbc_act[:, :, :d_inner].reshape(n_batch, seq_len, n_heads, d_inner // n_heads)
    b_mat = xbc_act[:, :, d_inner:d_inner + group_w].reshape(n_batch, seq_len, n_groups, STATE_DIM)
    c_mat = xbc_act[:, :, d_inner + group_w:].reshape(n_batch, seq_len, n_groups, STATE_DIM)
    dt_heads = jax.nn.softplus(proj_out[:, :, d_inner + conv_dim:].astype(jnp.float32) + dt_bias)
    y_heads = ssd_chunks(x_heads, dt_heads, dt_heads * -jnp.exp(a_log), b_mat, c_mat) + d_skip[:, None] * x_heads
    z_act = jax.nn.silu(proj_out[:, :, :d_inner].astype(jnp.float32))
    gated_y = y_heads.reshape(n_batch, seq_len, n_groups, -1) * z_act.reshape(n_batch, seq_len, n_groups, -1)
    normed = gated_y * lax.rsqrt(jnp.mean(jnp.square(gated_y), axis=-1, keepdims=True) + NORM_EPS)
    return (normed.reshape(n_batch, seq_len, d_inner) * gate_w.astype(jnp.float32)).astype(jnp.bfloat16)


def layer_forward(u_rows, params):
    norm_w, w_in, conv_w, conv_b, dt_bias, a_log, d_skip, gate_w, w_out = params
    h_norm, norm_pull = jax.vjp(pre_norm, u_rows, norm_w)
    proj_out = jnp.einsum('bld,dk->blk', h_norm, w_in, preferred_element_type=jnp.float32).astype(jnp.bfloat16)
    y_norm, core_pull = jax.vjp(mixer_core, proj_out, conv_w, conv_b, dt_bias, a_log, d_skip, gate_w)
    mixed = jnp.einsum('blk,kd->bld', y_norm, w_out, preferred_element_type=jnp.float32)
    out_rows = (u_rows.astype(jnp.float32) + mixed).astype(jnp.bfloat16)
    return out_rows, (h_norm, y_norm, norm_pull, core_pull)


def layer_backward(d_out, saved, w_in, w_out):
    h_norm, y_norm, norm_pull, core_pull = saved
    g_w_out = jnp.einsum('blk,bld->kd', y_norm, d_out, preferred_element_type=jnp.float32)
    d_ynorm = jnp.einsum('bld,kd->blk', d_out, w_out, preferred_element_type=jnp.float32).astype(jnp.bfloat16)
    d_proj, g_conv_w, g_conv_b, g_dt_bias, g_a_log, g_d_skip, g_gate_w = core_pull(d_ynorm)
    g_w_in = jnp.einsum('bld,blk->dk', h_norm, d_proj, preferred_element_type=jnp.float32)
    d_h = jnp.einsum('blk,dk->bld', d_proj, w_in, preferred_element_type=jnp.float32).astype(jnp.bfloat16)
    d_u_norm, g_norm_w = norm_pull(d_h)
    d_u = (d_out.astype(jnp.float32) + d_u_norm.astype(jnp.float32)).astype(jnp.bfloat16)
    return d_u, (g_norm_w, g_w_in, g_conv_w, g_conv_b, g_dt_bias, g_a_log, g_d_skip, g_gate_w, g_w_out)


def solution(mesh):
    dp_size = mesh.shape['dp']
    fsdp_size = mesh.shape['fsdp']
    act_spec = P(('dp', 'fsdp'), None, None)
    weight_specs = (P(None, 'fsdp'), P(None, 'fsdp', None), P(None, None, 'fsdp'), P(None, 'fsdp'), P(None, 'fsdp'), P(None, 'fsdp'), P(None, 'fsdp'), P(None, 'fsdp'), P(None, 'fsdp', None))

    def per_device(u_loc, g_loc, *pieces):
        batch_tot = u_loc.shape[0] * dp_size * fsdp_size

        def gather_layer(layer):
            return tuple(lax.all_gather(piece[layer], 'fsdp', axis=axis_id, tiled=True) for piece, axis_id in zip(pieces, GATHER_AXES))

        def gather_big(layer):
            w_in = lax.all_gather(pieces[1][layer], 'fsdp', axis=0, tiled=True)
            w_out = lax.all_gather(pieces[8][layer], 'fsdp', axis=0, tiled=True)
            return w_in, w_out

        def reduce_layer(grads):
            out_pieces = []
            for grad, piece, axis_id in zip(grads, pieces, GATHER_AXES):
                part_g = (grad.astype(jnp.float32) / batch_tot).astype(piece.dtype)
                summed = lax.psum_scatter(part_g, 'fsdp', scatter_dimension=axis_id, tiled=True)
                out_pieces.append(lax.psum(summed.astype(jnp.float32), 'dp'))
            return out_pieces

        full_one = gather_layer(0)
        hidden, saved_one = layer_forward(u_loc, full_one)
        full_two = gather_layer(1)
        out_loc, saved_two = layer_forward(hidden, full_two)
        in_two, out_two = gather_big(1)
        d_hidden, grads_two = layer_backward(g_loc, saved_two, in_two, out_two)
        pieces_two = reduce_layer(grads_two)
        in_one, out_one = gather_big(0)
        d_u, grads_one = layer_backward(d_hidden, saved_one, in_one, out_one)
        pieces_one = reduce_layer(grads_one)
        stacked = tuple(jnp.stack([first, second]) for first, second in zip(pieces_one, pieces_two))
        return (out_loc, d_u) + stacked

    return jax.shard_map(per_device, mesh=mesh, in_specs=(act_spec, act_spec) + weight_specs, out_specs=(act_spec, act_spec) + weight_specs, check_vma=False)
```

profile of v0, /device:TPU:0, one launch (start us, length us, event | category | flops | bytes accessed | tf_op | source)
XLA Modules:
  0.0 5424.9 jit_solution(8605132236831739923)
XLA Ops:
  55.8 50.8 all-gather.3
  106.7 112.9 %fusion.271 = (f32[5376]{0:T(1024)S(1)}, f32[5376]{0:T(1024)S(1)}, f32[5376]{0:T(1024)S(1)}, f32[5376]{0:T(1024)S(1)}) fusion(bf16[1,4,5376]{1,0,2:T(2,128)(2,1)S(1)} %all-gather.3), kind=kLoop, calls=%fused_computation.351 | loop fusion | flops 21504 | bytes 129024 | tf_op jit(solution)/shard_map/jvp()/convert_element_type | solution.py:56
  269.8 50.7 all-gather.12
  320.5 112.8 %fusion.267 = (f32[5376]{0:T(1024)}, f32[5376]{0:T(1024)}, f32[5376]{0:T(1024)}, f32[5376]{0:T(1024)}) fusion(bf16[1,4,5376]{1,0,2:T(2,128)(2,1)S(1)} %all-gather.12), kind=kLoop, calls=%fused_computation.343 | loop fusion | flops 21504 | bytes 129024 | tf_op jit(solution)/shard_map/jvp()/convert_element_type | solution.py:56
  435.2 66.9 %convert_bitcast_fusion.1 = bf16[1,1024,10576]{1,2,0:T(8,128)(2,1)} fusion(bf16[1,2560,10576]{1,2,0:T(8,128)(2,1)} %all-gather.23.cloned.1.call-done, bf16[1,1024,2560]{2,1,0:T(8,128)(2,1)} %param.12, f32[2560]{0:T(1024)S(1)} %convert_reduce_fusion.1, f32[1024]{0:T(1024)S(1)} %fusion.390), kind=kOutput, calls=%fused_computation.129 | convolution fusion | flops 55470014464 | bytes 81065984 | tf_op jit(solution)/shard_map/bld,dk->blk/dot_general | solution.py:72
  822.7 50.8 all-gather.27.cloned.1.call-done
  873.5 67.0 %convert_bitcast_fusion = bf16[1,1024,10576]{1,2,0:T(8,128)(2,1)} fusion(bf16[1,2560,10576]{1,2,0:T(8,128)(2,1)} %all-gather.27.cloned.1.call-done, bf16[1,1024,2560]{2,1,0:T(8,128)(2,1)} %get-tuple-element.168, f32[2560]{0:T(1024)S(1)} %copy-done.96, f32[1024]{0:T(1024)S(1)} %fusion.391), kind=kOutput, calls=%fused_computation.128 | convolution fusion | flops 55470014464 | bytes 81065984 | tf_op jit(solution)/shard_map/bld,dk->blk/dot_general | solution.py:72
  1212.0 56.3 %fusion.117 = (f32[1024]{0:T(1024)S(1)}, f32[1024]{0:T(1024)S(1)}, f32[1,1024,5120]{1,2,0:T(8,128)}, f32[1,1024,5120]{1,2,0:T(8,128)}, bf16[1024,5120]{0,1:T(8,128)(2,1)}) fusion(f32[5120]{0:T(1024)S(1)} %bitcast.769, bf16[1,1024,10576]{1,2,0:T(8,128)(2,1)} %convert_bitcast_fusion, f32[1,1024,5120]{1,2,0:T(8,128)} %reshape.2028, ...), kind=kOutput, calls=%fused_computation.190 | convolution fusion | flops 26922188800 | bytes 136364032 | tf_op jit(solution)/shard_map/bld,kd->blk/dot_general | solution.py:82
  1359.0 46.3 fusion.116
  1416.4 69.1 %fusion.21 = (f32[4,80,256]{2,1,0:T(8,128)S(1)}, f32[4,80,256]{2,1,0:T(8,128)}, bf16[4,256,256]{2,1,0:T(8,128)(2,1)S(1)}) fusion(f32[4,80,256]{2,1,0:T(8,128)S(1)} %copy-done.48, f32[4,256,256]{2,1,0:T(8,128)S(1)} %copy-done.41, pred[256,256]{1,0:T(8,128)(4,1)S(1)} %copy-done.86, f32[4,256,80,64]{1,2,3,0:T(8,128)} %copy_multiply_fusion.2, ...), kind=kOutput, calls=%fused_computation.28 | convolution fusion | flops 2914615296 | bytes 44564480 | tf_op jit(solution)/shard_map/transpose(jvp(bcgrqs,bcsgrp->bcqgrp))/dot_general | solution.py:33
  1711.9 47.7 multiply_reduce_fusion.2
  1759.6 47.8 fusion.66
  1849.7 83.1 %fusion.151 = (bf16[2560]{0:T(1024)(128)(2,1)}, f32[1024]{0:T(1024)S(1)}, bf16[1024,2560]{1,0:T(8,128)(2,1)}) fusion(bf16[1,1024,2560]{2,1,0:T(8,128)(2,1)} %get-tuple-element.168, f32[1024]{0:T(1024)S(1)} %copy-done.125, f32[2560]{0:T(1024)S(1)} %copy-done.97, bf16[1,2560,10576]{1,2,0:T(8,128)(2,1)} %all-gather.27.cloned.1.call-done, ...), kind=kOutput, calls=%fused_computation.263 | convolution fusion | flops 55537266688 | bytes 86318080 | tf_op jit(solution)/shard_map/blk,dk->bld/dot_general | solution.py:85
  2128.5 69.5 %fusion.23 = (f32[4,80,256]{2,1,0:T(8,128)}, f32[4,80,256]{2,1,0:T(8,128)}, bf16[4,256,256]{2,1,0:T(8,128)(2,1)S(1)}) fusion(f32[4,80,256]{2,1,0:T(8,128)S(1)} %copy-done.46, f32[4,256,256]{2,1,0:T(8,128)S(1)} %copy-done.39, pred[256,256]{1,0:T(8,128)(4,1)S(1)} %copy-done.87, f32[4,256,80,64]{1,2,3,0:T(8,128)} %copy_multiply_fusion.3, ...), kind=kOutput, calls=%fused_computation.30 | convolution fusion | flops 2914615296 | bytes 44564480 | tf_op jit(solution)/shard_map/transpose(jvp(bcgrqs,bcsgrp->bcqgrp))/dot_general | solution.py:33
  2400.6 47.2 multiply_reduce_fusion.3
  2447.8 48.0 fusion.58
  2573.0 75.1 %multiply_convert_fusion = bf16[2560,10576]{0,1:T(8,128)(2,1)} fusion(bf16[1,1024,5376]{1,2,0:T(8,128)(2,1)} %pad_add_fusion.5, bf16[1,1024,80]{1,2,0:T(8,128)(2,1)S(1)} %copy-done.75, bf16[1,1024,5120]{1,2,0:T(8,128)(2,1)} %get-tuple-element.117, bf16[1,1024,2560]{2,1,0:T(8,128)(2,1)} %get-tuple-element.168, f32[2560]{0:T(1024)S(1)} %copy-done.98, ...), kind=kOutput, calls=%fused_computation | convolution fusion | flops 55578312704 | bytes 81065984 | tf_op jit(solution)/shard_map/bld,blk->dk/dot_general | solution.py:84
  2648.0 67.9 %copy.486 = bf16[2560,10576]{1,0:T(8,128)(2,1)} copy(bf16[2560,10576]{0,1:T(8,128)(2,1)} %multiply_convert_fusion) | data formatting | bytes 108298240
  2759.1 75.1 %multiply_convert_fusion.1 = bf16[2560,10576]{0,1:T(8,128)(2,1)} fusion(bf16[1,1024,5376]{1,2,0:T(8,128)(2,1)} %pad_add_fusion.2, bf16[1,1024,80]{1,2,0:T(8,128)(2,1)S(1)} %copy-done.76, bf16[1,1024,5120]{1,2,0:T(8,128)(2,1)} %get-tuple-element.115, bf16[1,1024,2560]{2,1,0:T(8,128)(2,1)} %param.12, f32[2560]{0:T(1024)S(1)} %copy-done.95, ...), kind=kOutput, calls=%fused_computation.1 | convolution fusion | flops 55578312704 | bytes 81065984 | tf_op jit(solution)/shard_map/bld,blk->dk/dot_general | solution.py:84
  2834.2 70.2 %copy.484 = bf16[2560,10576]{1,0:T(8,128)(2,1)} copy(bf16[2560,10576]{0,1:T(8,128)(2,1)} %multiply_convert_fusion.1) | data formatting | bytes 108298240
  2907.2 82.5 %fusion.153 = (bf16[2560]{0:T(1024)(128)(2,1)S(1)}, f32[1024]{0:T(1024)S(1)}, bf16[1024,2560]{1,0:T(8,128)(2,1)}) fusion(bf16[1,1024,2560]{2,1,0:T(8,128)(2,1)} %param.12, f32[1024]{0:T(1024)S(1)} %copy-done.123, f32[2560]{0:T(1024)S(1)} %copy-done.95, bf16[1,2560,10576]{1,2,0:T(8,128)(2,1)} %all-gather.23.cloned.1.call-done, ...), kind=kOutput, calls=%fused_computation.265 | convolution fusion | flops 55537266688 | bytes 86318080 | tf_op jit(solution)/shard_map/blk,dk->bld/dot_general | solution.py:85
  3038.5 203.8 %reduce-scatter.21.cloned.1.call-done = bf16[640,10576]{1,0:T(8,128)(2,1)} async-done(((bf16[2560,10576]{1,0:T(8,128)(2,1)}), bf16[640,10576]{1,0:T(8,128)(2,1)}) %reduce-scatter.21.cloned.1.call-update) | async-done | bytes 13537296
  3273.4 321.7 %reduce-scatter.19.cloned.1.call-done = bf16[640,10576]{1,0:T(8,128)(2,1)} async-done(((bf16[2560,10576]{1,0:T(8,128)(2,1)}), bf16[640,10576]{1,0:T(8,128)(2,1)}) %reduce-scatter.19.cloned.1.call-update) | async-done | bytes 13537296
  3684.6 1677.8 %all-reduce.65.cloned.1.call-done = (f32[1,640,10576]{1,2,0:T(8,128)}, f32[1,640,10576]{1,2,0:T(8,128)}, f32[1,1280,2560]{2,1,0:T(8,128)}, f32[1,1280,2560]{2,1,0:T(8,128)}) async-done(((f32[1,640,10576]{1,2,0:T(8,128)}, f32[1,640,10576]{1,2,0:T(8,128)}, f32[1,1280,2560]{2,1,0:T(8,128)}, f32[1,1280,2560]{2,1,0:T(8,128)}), (f32[1,640,10576]{1,2,0:T(8,128)}, f32[1,640,10576]{1,2,0:T(8,128)}, ...) | async-done | bytes 80363536 | tf_op jit(solution)/shard_map/psum | solution.py:113
  (666 shorter events, 1803.1 us)
Async XLA Ops:
  7.2 428.0 %all-gather.23.cloned.1.call-start = ((), (), s32[]{:S(2)}) async-start(), calls=%async_computation.8 | async-start | bytes 67686400 | tf_op jit(solution)/shard_map/all_gather | solution.py:101
  27.7 755.9 %all-gather.25.cloned.1.call-start = ((), (), s32[]{:S(2)}) async-start(), calls=%async_computation.9 | async-start | bytes 32768000 | tf_op jit(solution)/shard_map/all_gather | solution.py:101
  38.0 195.9 %copy-start.157 = (f32[2,20]{1,0:T(2,128)S(1)}, f32[2,20]{1,0:T(2,128)}, u32[]{:S(2)}) copy-start(f32[2,20]{1,0:T(2,128)} %param.18) | copy-start | bytes 484
  38.1 196.1 %copy-start.158 = (f32[2,20]{1,0:T(2,128)S(1)}, f32[2,20]{1,0:T(2,128)}, u32[]{:S(2)}) copy-start(f32[2,20]{1,0:T(2,128)} %param.19) | copy-start | bytes 484
  38.1 196.3 %copy-start.159 = (f32[2,20]{1,0:T(2,128)S(1)}, f32[2,20]{1,0:T(2,128)}, u32[]{:S(2)}) copy-start(f32[2,20]{1,0:T(2,128)} %param.20) | copy-start | bytes 484
  38.1 204.6 %copy-start.120 = (bf16[2,1280]{1,0:T(2,128)(2,1)S(1)}, bf16[2,1280]{1,0:T(2,128)(2,1)}, u32[]{:S(2)}) copy-start(bf16[2,1280]{1,0:T(2,128)(2,1)} %param.21) | copy-start | bytes 15364
  38.1 835.4 %all-gather.27.cloned.1.call-start = ((), (), s32[]{:S(2)}) async-start(), calls=%async_computation.10 | async-start | bytes 67686400 | tf_op jit(solution)/shard_map/all_gather | solution.py:101
  38.8 1173.2 %all-gather.29.cloned.1.call-start = ((), (), s32[]{:S(2)}) async-start(), calls=%async_computation.11 | async-start | bytes 32768000 | tf_op jit(solution)/shard_map/all_gather | solution.py:101
  39.4 2977.4 %reduce-scatter.25.cloned.1.call-start = ((), (), s32[]{:S(2)}) async-start(), calls=%async_computation.15 | async-start | bytes 1720320
  50.7 451.4 %copy-start.94 = (f32[2560]{0:T(1024)}, f32[2560]{0:T(1024)S(1)}, u32[]{:S(2)}) copy-start(f32[2560]{0:T(1024)S(1)} %convert_reduce_fusion.1) | copy-start | bytes 30724
  54.3 447.8 %copy-start.122 = (f32[1024]{0:T(1024)}, f32[1024]{0:T(1024)S(1)}, u32[]{:S(2)}) copy-start(f32[1024]{0:T(1024)S(1)} %fusion.390) | copy-start | bytes 12292
  219.6 292.7 %copy-start.49 = (f32[5376]{0:T(1024)}, f32[5376]{0:T(1024)S(1)}, u32[]{:S(2)}) copy-start(f32[5376]{0:T(1024)S(1)} %get-tuple-element.45) | copy-start | bytes 64516
  219.6 292.7 %copy-start.51 = (f32[5376]{0:T(1024)}, f32[5376]{0:T(1024)S(1)}, u32[]{:S(2)}) copy-start(f32[5376]{0:T(1024)S(1)} %get-tuple-element.46) | copy-start | bytes 64516
  219.6 292.7 %copy-start.53 = (f32[5376]{0:T(1024)}, f32[5376]{0:T(1024)S(1)}, u32[]{:S(2)}) copy-start(f32[5376]{0:T(1024)S(1)} %get-tuple-element.47) | copy-start | bytes 64516
  219.6 292.7 %copy-start.55 = (f32[5376]{0:T(1024)}, f32[5376]{0:T(1024)S(1)}, u32[]{:S(2)}) copy-start(f32[5376]{0:T(1024)S(1)} %get-tuple-element.48) | copy-start | bytes 64516
  241.4 260.7 %copy-start.151 = (f32[80]{0:T(128)}, f32[80]{0:T(128)S(1)}, u32[]{:S(2)}) copy-start(f32[80]{0:T(128)S(1)} %get-tuple-element.66) | copy-start | bytes 964
  241.4 260.7 %copy-start.155 = (f32[80]{0:T(128)}, f32[80]{0:T(128)S(1)}, u32[]{:S(2)}) copy-start(f32[80]{0:T(128)S(1)} %get-tuple-element.65) | copy-start | bytes 964
  2383.3 634.6 %reduce-scatter.23.cloned.1.call-start = ((), (), s32[]{:S(2)}) async-start(), calls=%async_computation.14 | async-start | bytes 1720320
  2497.7 522.1 %reduce-scatter.17.cloned.1.call-start = ((), (), s32[]{:S(2)}) async-start(), calls=%async_computation.7 | async-start | bytes 32768000 | tf_op jit(solution)/shard_map/reduce_scatter | solution.py:112
  2534.6 494.5 %reduce-scatter.15.cloned.1.call-start = ((), (), s32[]{:S(2)}) async-start(), calls=%async_computation.6 | async-start | bytes 32768000 | tf_op jit(solution)/shard_map/reduce_scatter | solution.py:112
  2572.1 670.2 %reduce-scatter.21.cloned.1.call-start = ((), (), s32[]{:S(2)}) async-start(), calls=%async_computation.13 | async-start | bytes 67993600
  2716.0 879.1 %reduce-scatter.19.cloned.1.call-start = ((), (), s32[]{:S(2)}) async-start(), calls=%async_computation.12 | async-start | bytes 67993600
  2904.4 771.2 %all-reduce.63.cloned.1.call-start = ((), (), s32[]{:S(2)}) async-start(), calls=%async_computation.16 | async-start | bytes 149504 | tf_op jit(solution)/shard_map/psum | solution.py:113
  3019.7 2342.6 %all-reduce.65.cloned.1.call-start = ((), (), s32[]{:S(2)}) async-start(), calls=%async_computation.17 | async-start | bytes 160727040 | tf_op jit(solution)/shard_map/psum | solution.py:113
  (152 other events, 5561.9 us)
Sparse Core Ops, SparseCore 0:
  27.8 366.4 all-gather.22
  395.8 158.6 all-gather.24
  556.1 317.3 all-gather.26
  874.9 158.6 all-gather.28
  2383.4 21.1 reduce-scatter.24
  2497.8 21.1 reduce-scatter.22
  2534.8 175.3 reduce-scatter.16
  2712.7 175.3 reduce-scatter.14
  2890.7 351.5 reduce-scatter.20
  3244.7 350.3 reduce-scatter.18
  3599.4 17.4 all-reduce.62
  3626.4 1735.8 all-reduce.64
where the time goes:
time: 5440 us; the launch traced here: 5420 us
  waiting for transfers between devices  2260 us (42%)
  matrix products  1200 us (22%)
  other arithmetic  1020 us (19%)
  local copies, waits for them, and re-layouts  758 us (14%)
  blocking collectives  173 us (3%)
    psum x2, waiting for transfers between devices, reduce_layer(): out_pieces.append(lax.psum(summed.astype(jnp.float32), 'dp'))  1680 us
    unnamed x16, waiting for transfers between devices  527 us
    dot_general x6, matrix products, ssd_chunks(): jnp.einsum('bcgrqs,bcsgrp->bcqgrp', scores[:, :, :, None] * decay_mat, x_...  270 us
    convert_element_type x2, other arithmetic, mixer_core(): conv_w[tap].astype(jnp.float32)  226 us
    unnamed x361, local copies, waits for them, and re-layouts  225 us
    dot_general x2, matrix products, layer_backward(): jnp.einsum('blk,dk->bld', d_proj, w_in, preferred_element_type=jnp.float32)  166 us
    dot_general x2, matrix products, layer_backward(): jnp.einsum('bld,blk->dk', h_norm, d_proj, preferred_element_type=jnp.floa...  150 us
    all_gather x6, blocking collectives, gather_layer(): lax.all_gather(piece[layer], 'fsdp', axis=axis_id, tiled=True)  136 us
  transfers between devices with their start and end apart: 12, of which 4 were waited for; matrix products, arithmetic and copies ran while one was open for 32% of the time, Pallas kernels for 0%

commit v1 on v0

v1 whole, which is shorter than its diff:
```python
import functools

import jax
import jax.numpy as jnp
from jax import lax
from jax.experimental import pallas as pl
from jax.experimental.layout import Layout, with_layout_constraint
from jax.experimental.pallas import tpu as pltpu
from jax.sharding import PartitionSpec as P

CHUNK_LEN = 256
STATE_DIM = 128
HEAD_DIM = 64
HEADS_BLK = 8
LANES_BLK = HEADS_BLK * HEAD_DIM
NORM_EPS = 1e-5
F32 = jnp.float32
BF16 = jnp.bfloat16


def row_major(arr):
    return with_layout_constraint(arr, Layout(major_to_minor=tuple(range(arr.ndim))))


def dot_nn(a, b):
    return lax.dot_general(a, b, (((1,), (0,)), ((), ())), preferred_element_type=F32)


def dot_nt(a, b):
    return lax.dot_general(a, b, (((1,), (1,)), ((), ())), preferred_element_type=F32)


def dot_tn(a, b):
    return lax.dot_general(a, b, (((0,), (0,)), ((), ())), preferred_element_type=F32)


def spread_heads(cols, lane):
    rows = cols.shape[0]
    parts = []
    for pair in range(HEADS_BLK // 2):
        left = jnp.broadcast_to(cols[:, 2 * pair:2 * pair + 1], (rows, 128))
        right = jnp.broadcast_to(cols[:, 2 * pair + 1:2 * pair + 2], (rows, 128))
        parts.append(jnp.where(lane[:rows] < HEAD_DIM, left, right))
    return jnp.concatenate(parts, axis=1)


def head_sums(vals, seg):
    hi = vals.astype(BF16)
    rest = vals - hi.astype(F32)
    mid = rest.astype(BF16)
    low = (rest - mid.astype(F32)).astype(BF16)
    return dot_nn(hi, seg) + dot_nn(mid, seg) + dot_nn(low, seg)


def ssd_fwd_kernel(x_ref, b_ref, c_ref, dt_ref, cum_ref, cumt_ref, skip_ref, y_ref, prev_ref, state, scores):
    chunk = pl.program_id(0)
    blk = pl.program_id(1)
    b_mat = b_ref[...].astype(BF16)
    c_mat = c_ref[...].astype(BF16)

    @pl.when(chunk == 0)
    def _():
        state[blk] = jnp.zeros((STATE_DIM, LANES_BLK), F32)

    @pl.when(blk == 0)
    def _():
        scores[...] = dot_nt(c_mat, b_mat)

    lane = lax.broadcasted_iota(jnp.int32, (CHUNK_LEN, 128), 1)
    causal = lax.broadcasted_iota(jnp.int32, (CHUNK_LEN, CHUNK_LEN), 0) >= lax.broadcasted_iota(jnp.int32, (CHUNK_LEN, CHUNK_LEN), 1)
    x_blk = x_ref[...]
    cum = cum_ref[0]
    cum_e = spread_heads(cum, lane)
    tot_e = cum_e[CHUNK_LEN - 1:CHUNK_LEN, :]
    x_dt = x_blk * spread_heads(dt_ref[0], lane)
    xd_b = x_dt.astype(BF16)
    prev = state[blk]
    prev_ref[0] = prev
    y_off = dot_nn(c_mat, prev.astype(BF16)) * jnp.exp(cum_e)
    state[blk] = prev * jnp.exp(tot_e) + dot_tn(b_mat, (x_dt * jnp.exp(tot_e - cum_e)).astype(BF16))
    g_mat = scores[...]
    zero = jnp.zeros((CHUNK_LEN, 128), BF16)
    for pair in range(HEADS_BLK // 2):
        cols = slice(pair * 128, pair * 128 + 128)
        acc = y_off[:, cols] + skip_ref[:, cols] * x_blk[:, cols]
        for side in range(2):
            head = 2 * pair + side
            gap = cum[:, head:head + 1] - cumt_ref[0][head:head + 1, :]
            decay = jnp.exp(jnp.where(causal, gap, -1e30))
            mine = (lane < HEAD_DIM) if side == 0 else (lane >= HEAD_DIM)
            acc = acc + dot_nn((g_mat * decay).astype(BF16), jnp.where(mine, xd_b[:, cols], zero))
        y_ref[:, cols] = acc


def ssd_bwd_kernel(dy_ref, y_ref, x_ref, b_ref, c_ref, dt_ref, cum_ref, cumt_ref, skip_ref, prev_ref,
                   dxbc_ref, dcum_ref, ddt_ref, dskip_ref, d_state, scores_t, dg_t, d_b, d_c, *, n_blk):
    rev = pl.program_id(0)
    blk = pl.program_id(1)
    b_mat = b_ref[...].astype(BF16)
    c_mat = c_ref[...].astype(BF16)

    @pl.when(blk == 0)
    def _():
        scores_t[...] = dot_nt(b_mat, c_mat)
        dg_t[...] = jnp.zeros_like(dg_t)
        d_b[...] = jnp.zeros_like(d_b)
        d_c[...] = jnp.zeros_like(d_c)

    @pl.when((rev == 0) & (blk < n_blk))
    def _():
        d_state[blk] = jnp.zeros((STATE_DIM, LANES_BLK), F32)

    @pl.when(blk < n_blk)
    def _():
        lane = lax.broadcasted_iota(jnp.int32, (CHUNK_LEN, 128), 1)
        row = lax.broadcasted_iota(jnp.int32, (CHUNK_LEN, 128), 0)
        causal = lax.broadcasted_iota(jnp.int32, (CHUNK_LEN, CHUNK_LEN), 0) <= lax.broadcasted_iota(jnp.int32, (CHUNK_LEN, CHUNK_LEN), 1)
        seg = (lax.broadcasted_iota(jnp.int32, (LANES_BLK, 128), 0) // HEAD_DIM == lax.broadcasted_iota(jnp.int32, (LANES_BLK, 128), 1))
        seg = jnp.where(seg, 1.0, 0.0).astype(BF16)
        x_blk = x_ref[...]
        dy = dy_ref[...]
        cum = cum_ref[0]
        cum_e = spread_heads(cum, lane)
        tot_e = cum_e[CHUNK_LEN - 1:CHUNK_LEN, :]
        dt_e = spread_heads(dt_ref[0], lane)
        x_dt = x_blk * dt_e
        xd_b = x_dt.astype(BF16)
        dy_b = dy.astype(BF16)
        skip = skip_ref[...]
        prev = prev_ref[0]
        prev_b = prev.astype(BF16)
        d_next = d_state[blk]
        dn_b = d_next.astype(BF16)
        end_decay = jnp.exp(tot_e - cum_e)
        dy_in = (dy * jnp.exp(cum_e)).astype(BF16)
        tail = dot_nn(b_mat, dn_b) * end_decay
        d_b[...] += dot_nt((x_dt * end_decay).astype(BF16), dn_b)
        d_c[...] += dot_nt(dy_in, prev_b)
        d_state[blk] = d_next * jnp.exp(tot_e) + dot_tn(c_mat, dy_in)
        r_in = x_dt * tail
        tot_grad = jnp.sum(r_in, axis=0, keepdims=True) + jnp.exp(tot_e) * jnp.sum(prev * d_next, axis=0, keepdims=True)
        g_t = scores_t[...]
        zero = jnp.zeros((CHUNK_LEN, 128), BF16)
        dg_sum = None
        diag_parts = []
        for pair in range(HEADS_BLK // 2):
            cols = slice(pair * 128, pair * 128 + 128)
            acc = None
            for side in range(2):
                head = 2 * pair + side
                gap = cumt_ref[0][head:head + 1, :] - cum[:, head:head + 1]
                decay = jnp.exp(jnp.where(causal, gap, -1e30))
                mine = (lane < HEAD_DIM) if side == 0 else (lane >= HEAD_DIM)
                dy_m = jnp.where(mine, dy_b[:, cols], zero)
                part = dot_nn((g_t * decay).astype(BF16), dy_m)
                acc = part if acc is None else acc + part
                dg = dot_nt(xd_b[:, cols], dy_m) * decay
                dg_sum = dg if dg_sum is None else dg_sum + dg
            diag_parts.append(acc)
        dg_t[...] += dg_sum
        diag = jnp.concatenate(diag_parts, axis=1)
        d_xdt = diag + tail
        y_ssd = y_ref[...] - skip * x_blk
        dxbc_ref[...] = d_xdt * dt_e + skip * dy
        ddt_ref[...] = head_sums(d_xdt * x_blk, seg)
        flow = dy_b.astype(F32) * y_ssd - xd_b.astype(F32) * diag - r_in
        last = lax.broadcasted_iota(jnp.int32, (CHUNK_LEN, LANES_BLK), 0) == CHUNK_LEN - 1
        flow = flow + jnp.where(last, jnp.broadcast_to(tot_grad, flow.shape), 0.0)
        dcum_ref[...] = head_sums(flow, seg)
        dskip_ref[0] = jnp.sum((dy * x_blk).reshape(CHUNK_LEN // 8, 8, LANES_BLK), axis=0)

    @pl.when(blk == n_blk)
    def _():
        dg_b = dg_t[...].astype(BF16)
        dxbc_ref[:, :STATE_DIM] = d_b[...] + dot_nn(dg_b, c_mat)
        dxbc_ref[:, STATE_DIM:2 * STATE_DIM] = d_c[...] + dot_tn(dg_b, b_mat)
        dxbc_ref[:, 2 * STATE_DIM:] = jnp.zeros((CHUNK_LEN, LANES_BLK - 2 * STATE_DIM), F32)


def head_tables(dt_heads, a_heads):
    seq_len, n_heads = dt_heads.shape
    n_chunks = seq_len // CHUNK_LEN
    lower = jnp.tril(jnp.ones((CHUNK_LEN, CHUNK_LEN), F32))
    cum = jnp.einsum('qs,csh->cqh', lower, a_heads.reshape(n_chunks, CHUNK_LEN, n_heads), precision=lax.Precision.HIGHEST)
    cum = cum.reshape(seq_len, n_heads // HEADS_BLK, HEADS_BLK)
    dt_blk = dt_heads.reshape(seq_len, n_heads // HEADS_BLK, HEADS_BLK).transpose(1, 0, 2)
    return dt_blk, cum.transpose(1, 0, 2), cum.transpose(1, 2, 0)


def ssd_forward(xbc_act, dt_blk, cum_blk, cum_t, skip_row):
    seq_len = xbc_act.shape[0]
    n_blk = dt_blk.shape[0]
    d_inner = n_blk * LANES_BLK
    n_chunks = seq_len // CHUNK_LEN
    b_col = d_inner // STATE_DIM
    return pl.pallas_call(
        ssd_fwd_kernel,
        grid=(n_chunks, n_blk),
        in_specs=[
            pl.BlockSpec((CHUNK_LEN, LANES_BLK), lambda c, h: (c, h)),
            pl.BlockSpec((CHUNK_LEN, STATE_DIM), lambda c, h: (c, b_col)),
            pl.BlockSpec((CHUNK_LEN, STATE_DIM), lambda c, h: (c, b_col + 1)),
            pl.BlockSpec((1, CHUNK_LEN, HEADS_BLK), lambda c, h: (h, c, 0)),
            pl.BlockSpec((1, CHUNK_LEN, HEADS_BLK), lambda c, h: (h, c, 0)),
            pl.BlockSpec((1, HEADS_BLK, CHUNK_LEN), lambda c, h: (h, 0, c)),
            pl.BlockSpec((1, LANES_BLK), lambda c, h: (0, h)),
        ],
        out_specs=[
            pl.BlockSpec((CHUNK_LEN, LANES_BLK), lambda c, h: (c, h)),
            pl.BlockSpec((1, STATE_DIM, LANES_BLK), lambda c, h: (c, 0, h)),
        ],
        out_shape=[
            jax.ShapeDtypeStruct((seq_len, d_inner), F32),
            jax.ShapeDtypeStruct((n_chunks, STATE_DIM, d_inner), F32),
        ],
        scratch_shapes=[
            pltpu.VMEM((n_blk, STATE_DIM, LANES_BLK), F32),
            pltpu.VMEM((CHUNK_LEN, CHUNK_LEN), F32),
        ],
        compiler_params=pltpu.CompilerParams(dimension_semantics=('arbitrary', 'arbitrary'), vmem_limit_bytes=40 * 2**20),
        cost_estimate=pl.CostEstimate(flops=60_000_000_000, bytes_accessed=50_000_000, transcendentals=0),
        name='ssd_forward',
    )(xbc_act, xbc_act, xbc_act, dt_blk, cum_blk, cum_t, skip_row)


def ssd_backward(dy, y_all, xbc_act, dt_blk, cum_blk, cum_t, skip_row, prev_states):
    seq_len, conv_dim = xbc_act.shape
    n_blk = dt_blk.shape[0]
    d_inner = n_blk * LANES_BLK
    n_chunks = seq_len // CHUNK_LEN
    b_col = d_inner // STATE_DIM
    top = n_chunks - 1
    cap = n_blk - 1
    wide = pl.BlockSpec((CHUNK_LEN, LANES_BLK), lambda c, h: (top - c, jnp.minimum(h, cap)))
    table = pl.BlockSpec((1, CHUNK_LEN, HEADS_BLK), lambda c, h: (jnp.minimum(h, cap), top - c, 0))
    sums = pl.BlockSpec((CHUNK_LEN, 128), lambda c, h: (top - c, jnp.minimum(h, cap)))
    return pl.pallas_call(
        functools.partial(ssd_bwd_kernel, n_blk=n_blk),
        grid=(n_chunks, n_blk + 1),
        in_specs=[
            wide, wide, wide,
            pl.BlockSpec((CHUNK_LEN, STATE_DIM), lambda c, h: (top - c, b_col)),
            pl.BlockSpec((CHUNK_LEN, STATE_DIM), lambda c, h: (top - c, b_col + 1)),
            table, table,
            pl.BlockSpec((1, HEADS_BLK, CHUNK_LEN), lambda c, h: (jnp.minimum(h, cap), 0, top - c)),
            pl.BlockSpec((1, LANES_BLK), lambda c, h: (0, jnp.minimum(h, cap))),
            pl.BlockSpec((1, STATE_DIM, LANES_BLK), lambda c, h: (top - c, 0, jnp.minimum(h, cap))),
        ],
        out_specs=[
            pl.BlockSpec((CHUNK_LEN, LANES_BLK), lambda c, h: (top - c, h)),
            sums, sums,
            pl.BlockSpec((1, 8, LANES_BLK), lambda c, h: (top - c, 0, jnp.minimum(h, cap))),
        ],
        out_shape=[
            jax.ShapeDtypeStruct((seq_len, conv_dim), F32),
            jax.ShapeDtypeStruct((seq_len, n_blk * 128), F32),
            jax.ShapeDtypeStruct((seq_len, n_blk * 128), F32),
            jax.ShapeDtypeStruct((n_chunks, 8, d_inner), F32),
        ],
        scratch_shapes=[
            pltpu.VMEM((n_blk, STATE_DIM, LANES_BLK), F32),
            pltpu.VMEM((CHUNK_LEN, CHUNK_LEN), F32),
            pltpu.VMEM((CHUNK_LEN, CHUNK_LEN), F32),
            pltpu.VMEM((CHUNK_LEN, STATE_DIM), F32),
            pltpu.VMEM((CHUNK_LEN, STATE_DIM), F32),
        ],
        compiler_params=pltpu.CompilerParams(dimension_semantics=('arbitrary', 'arbitrary'), vmem_limit_bytes=40 * 2**20),
        cost_estimate=pl.CostEstimate(flops=150_000_000_000, bytes_accessed=100_000_000, transcendentals=0),
        name='ssd_backward',
    )(dy, y_all, xbc_act, xbc_act, xbc_act, dt_blk, cum_blk, cum_t, skip_row, prev_states)


def pre_norm(u_rows, norm_w):
    rows_f = u_rows.astype(F32)
    inv_rms = lax.rsqrt(jnp.mean(jnp.square(rows_f), axis=-1, keepdims=True) + NORM_EPS)
    return (rows_f * inv_rms * norm_w).astype(BF16)


def dt_part(dt_raw, dt_bias, a_log):
    dt_heads = jax.nn.softplus(dt_raw.astype(F32) + dt_bias)
    return dt_heads, dt_heads * -jnp.exp(a_log)


def delayed(vals, count, row):
    return vals if count == 0 else jnp.where(row >= count, pltpu.roll(vals, count, 0), 0.0)


def advanced(vals, count, row):
    seq_len = vals.shape[0]
    return vals if count == 0 else jnp.where(row < seq_len - count, pltpu.roll(vals, seq_len - count, 0), 0.0)


def conv_taps(p_ref, w_ref, bias_ref):
    x_cols = p_ref[...].astype(F32)
    row = lax.broadcasted_iota(jnp.int32, x_cols.shape, 0)
    n_taps = w_ref.shape[0]
    shifted = [delayed(x_cols, n_taps - 1 - tap, row) for tap in range(n_taps)]
    conv_out = bias_ref[...] + sum(shifted[tap] * w_ref[tap:tap + 1, :] for tap in range(n_taps))
    return row, shifted, conv_out


def conv_fwd_kernel(p_ref, w_ref, bias_ref, act_ref):
    _, _, conv_out = conv_taps(p_ref, w_ref, bias_ref)
    act_ref[...] = conv_out * jax.nn.sigmoid(conv_out)


def conv_bwd_kernel(p_ref, d_ref, w_ref, bias_ref, ddt_ref, dp_ref, gw_ref, *, n_cols):
    col = pl.program_id(0)

    @pl.when(col < n_cols)
    def _():
        row, shifted, conv_out = conv_taps(p_ref, w_ref, bias_ref)
        n_taps = len(shifted)
        sig = jax.nn.sigmoid(conv_out)
        d_conv = d_ref[...] * (sig * (1.0 + conv_out * (1.0 - sig)))
        d_p = sum(advanced(d_conv, n_taps - 1 - tap, row) * w_ref[tap:tap + 1, :] for tap in range(n_taps))
        dp_ref[...] = d_p.astype(BF16)
        rows = [jnp.sum(d_conv * part, axis=0, keepdims=True) for part in shifted]
        rows.append(jnp.sum(d_conv, axis=0, keepdims=True))
        rows.append(jnp.zeros((8 - len(rows), d_conv.shape[1]), F32))
        gw_ref[...] = jnp.concatenate(rows, axis=0)

    @pl.when(col == n_cols)
    def _():
        dp_ref[:, :128] = ddt_ref[...].astype(BF16)
        dp_ref[:, 128:] = jnp.zeros((dp_ref.shape[0], dp_ref.shape[1] - 128), BF16)


COLS_BLK = 256


def conv_forward(p_x, conv_w, conv_b):
    seq_len = p_x.shape[0]
    n_taps, conv_dim = conv_w.shape
    return pl.pallas_call(
        conv_fwd_kernel,
        grid=(conv_dim // COLS_BLK,),
        in_specs=[
            pl.BlockSpec((seq_len, COLS_BLK), lambda c: (0, c)),
            pl.BlockSpec((n_taps, COLS_BLK), lambda c: (0, c)),
            pl.BlockSpec((1, COLS_BLK), lambda c: (0, c)),
        ],
        out_specs=pl.BlockSpec((seq_len, COLS_BLK), lambda c: (0, c)),
        out_shape=jax.ShapeDtypeStruct((seq_len, conv_dim), F32),
        compiler_params=pltpu.CompilerParams(dimension_semantics=('arbitrary',), vmem_limit_bytes=40 * 2**20),
        cost_estimate=pl.CostEstimate(flops=20_000_000_000, bytes_accessed=33_000_000, transcendentals=0),
        name='conv_forward',
    )(p_x, conv_w, conv_b[None, :])


def conv_backward(p_x, d_act, conv_w, conv_b, d_dt_raw):
    seq_len, width = p_x.shape
    n_taps, conv_dim = conv_w.shape
    n_cols = conv_dim // COLS_BLK
    cap = n_cols - 1
    d_dt_raw = jnp.pad(d_dt_raw, ((0, 0), (0, 128 - d_dt_raw.shape[1])))
    return pl.pallas_call(
        functools.partial(conv_bwd_kernel, n_cols=n_cols),
        grid=(n_cols + 1,),
        in_specs=[
            pl.BlockSpec((seq_len, COLS_BLK), lambda c: (0, jnp.minimum(c, cap))),
            pl.BlockSpec((seq_len, COLS_BLK), lambda c: (0, jnp.minimum(c, cap))),
            pl.BlockSpec((n_taps, COLS_BLK), lambda c: (0, jnp.minimum(c, cap))),
            pl.BlockSpec((1, COLS_BLK), lambda c: (0, jnp.minimum(c, cap))),
            pl.BlockSpec((seq_len, 128), lambda c: (0, 0)),
        ],
        out_specs=[
            pl.BlockSpec((seq_len, COLS_BLK), lambda c: (0, c)),
            pl.BlockSpec((8, COLS_BLK), lambda c: (0, jnp.minimum(c, cap))),
        ],
        out_shape=[
            jax.ShapeDtypeStruct((seq_len, width), BF16),
            jax.ShapeDtypeStruct((8, conv_dim), F32),
        ],
        compiler_params=pltpu.CompilerParams(dimension_semantics=('arbitrary',), vmem_limit_bytes=40 * 2**20),
        cost_estimate=pl.CostEstimate(flops=50_000_000_000, bytes_accessed=44_000_000, transcendentals=0),
        name='conv_backward',
    )(p_x, d_act, conv_w, conv_b[None, :], d_dt_raw)


def gate_part(y_all, p_z, gate_w):
    gated_y = y_all * jax.nn.silu(p_z.astype(F32))
    normed = gated_y * lax.rsqrt(jnp.mean(jnp.square(gated_y), axis=-1, keepdims=True) + NORM_EPS)
    return (normed * gate_w).astype(BF16)


def layer_forward(u_rows, small, w_x, w_z, w_out):
    norm_w, conv_w, conv_b, dt_bias, a_log, d_skip, gate_w = small
    h_norm, norm_pull = jax.vjp(pre_norm, u_rows, norm_w)
    p_x = jnp.dot(h_norm, w_x, preferred_element_type=F32).astype(BF16)
    xbc_act = conv_forward(p_x, conv_w, conv_b)
    (dt_heads, a_heads), dt_pull = jax.vjp(dt_part, p_x[:, conv_w.shape[1]:].astype(F32), dt_bias, a_log)
    tables = head_tables(dt_heads, a_heads)
    skip_row = jnp.repeat(d_skip, HEAD_DIM)[None, :]
    y_all, prev_states = ssd_forward(xbc_act, *tables, skip_row)
    p_z = jnp.dot(h_norm, w_z, preferred_element_type=F32).astype(BF16)
    y_norm, gate_pull = jax.vjp(gate_part, y_all, p_z, gate_w)
    mixed = jnp.dot(y_norm, w_out, preferred_element_type=F32)
    out_rows = (u_rows.astype(F32) + mixed).astype(BF16)
    return out_rows, (h_norm, y_norm, norm_pull, p_x, dt_pull, gate_pull, xbc_act, tables, skip_row, y_all, prev_states)


def solution(mesh):
    dp_size = mesh.shape['dp']
    fsdp_size = mesh.shape['fsdp']
    act_spec = P(('dp', 'fsdp'), None, None)
    weight_specs = (P(None, 'fsdp'), P(None, 'fsdp', None), P(None, None, 'fsdp'), P(None, 'fsdp'), P(None, 'fsdp'), P(None, 'fsdp'), P(None, 'fsdp'), P(None, 'fsdp'), P(None, 'fsdp', None))
    swap = [(i, (i + 1) % dp_size) for i in range(dp_size)]

    def per_device(u_loc, g_loc, *pieces):
        batch_tot = u_loc.shape[0] * dp_size * fsdp_size
        small_ids = (0, 2, 3, 4, 5, 6, 7)
        d_inner = pieces[7].shape[1] * fsdp_size
        n_heads = pieces[4].shape[1] * fsdp_size

        packed = jnp.concatenate([pieces[i].astype(F32).reshape(-1) for i in small_ids])
        spread = lax.all_gather(packed, 'fsdp', axis=0, tiled=False)
        smalls = []
        offset = 0
        for i in small_ids:
            shape = pieces[i].shape
            count = pieces[i].size
            part = spread[:, offset:offset + count].reshape((fsdp_size,) + shape)
            part = jnp.moveaxis(part, 0, -2)
            smalls.append(part.reshape(shape[:-1] + (shape[-1] * fsdp_size,)))
            offset += count

        def gather(piece):
            return lax.all_gather(piece, 'fsdp', axis=0, tiled=True)

        w_full = []
        for layer in range(2):
            w_x = gather(pieces[1][layer, :, d_inner:])
            w_z = gather(pieces[1][layer, :, :d_inner])
            w_full.append((w_x, w_z, gather(pieces[8][layer])))

        def local_grad(lhs, rhs):
            grad = lax.dot_general(lhs, rhs, (((0,), (0,)), ((), ())), preferred_element_type=F32)
            return row_major((grad / batch_tot).astype(BF16))

        def scatter_sum(part_g):
            return lax.psum_scatter(part_g, 'fsdp', scatter_dimension=0, tiled=True)

        def dp_total(mine):
            total = mine.astype(F32)
            moving = mine
            for _ in range(dp_size - 1):
                moving = row_major(lax.ppermute(moving, 'dp', swap))
                total = total + moving.astype(F32)
            return row_major(total)

        def unpack(sums):
            return sums.reshape(sums.shape[0], -1, 128)[:, :, :HEADS_BLK].reshape(sums.shape[0], n_heads)

        def layer_backward(d_out, saved, weights, small, behind):
            h_norm, y_norm, norm_pull, p_x, dt_pull, gate_pull, xbc_act, tables, skip_row, y_all, prev_states = saved
            w_x, w_z, w_out = weights
            done = None
            g_out = local_grad(y_norm, d_out)
            d_out, g_out = lax.optimization_barrier((d_out, g_out))
            s_out = scatter_sum(g_out)
            d_ynorm = lax.dot_general(d_out, w_out, (((1,), (1,)), ((), ())), preferred_element_type=F32).astype(BF16)
            dy, d_pz, g_gate = gate_pull(d_ynorm)
            g_z = local_grad(h_norm, d_pz)
            if behind is not None:
                dy, g_z, s_z_old = lax.optimization_barrier((dy, g_z, behind[0]))
                t_z_old = dp_total(s_z_old)
            else:
                dy, g_z = lax.optimization_barrier((dy, g_z))
            s_z = row_major(scatter_sum(g_z).T)
            d_xbc, d_cum, d_dt, d_skip = ssd_backward(dy, y_all, xbc_act, *tables, skip_row, prev_states)
            if behind is not None:
                d_xbc, t_z_old, s_x_old, s_out = lax.optimization_barrier((d_xbc, t_z_old, behind[1], s_out))
                t_x_old = dp_total(s_x_old)
                t_out = dp_total(s_out)
            else:
                d_xbc, s_out = lax.optimization_barrier((d_xbc, s_out))
                t_out = dp_total(s_out)
            seq_len = dy.shape[0]
            n_chunks = seq_len // CHUNK_LEN
            upper = jnp.triu(jnp.ones((CHUNK_LEN, CHUNK_LEN), F32))
            d_a = jnp.einsum('qs,csh->cqh', upper, unpack(d_cum).reshape(n_chunks, CHUNK_LEN, n_heads), precision=lax.Precision.HIGHEST)
            d_dt_raw, g_dt_bias, g_a_log = dt_pull((unpack(d_dt), d_a.reshape(seq_len, n_heads)))
            d_px, g_conv = conv_backward(p_x, d_xbc, small[1], small[2], d_dt_raw)
            g_conv_w = g_conv[:small[1].shape[0]]
            g_conv_b = g_conv[small[1].shape[0]]
            g_x = local_grad(h_norm, d_px)
            if behind is not None:
                d_px, g_x, t_x_old, s_z = lax.optimization_barrier((d_px, g_x, t_x_old, s_z))
            else:
                d_px, g_x = lax.optimization_barrier((d_px, g_x))
            s_x = row_major(scatter_sum(g_x).T)
            d_h = lax.dot_general(d_pz, w_z, (((1,), (1,)), ((), ())), preferred_element_type=F32)
            d_h = (d_h + lax.dot_general(d_px, w_x, (((1,), (1,)), ((), ())), preferred_element_type=F32)).astype(BF16)
            d_u_norm, g_norm = norm_pull(d_h)
            d_u = (d_out.astype(F32) + d_u_norm.astype(F32)).astype(BF16)
            if behind is not None:
                done = (t_z_old, t_x_old)
            d_u, t_out = lax.optimization_barrier((d_u, t_out))
            g_skip = jnp.sum(jnp.sum(d_skip, axis=(0, 1)).reshape(n_heads, HEAD_DIM), axis=-1)
            small_g = (g_norm, g_conv_w, g_conv_b, g_dt_bias, g_a_log, g_skip, g_gate)
            return d_u, t_out, (s_z, s_x), done, small_g

        u_rows = u_loc[0]
        small_one = [s[0] for s in smalls]
        small_two = [s[1] for s in smalls]
        hidden, saved_one = layer_forward(u_rows, small_one, *w_full[0])
        out_rows, saved_two = layer_forward(hidden, small_two, *w_full[1])
        d_hidden, t_out_two, behind, _, sm_two = layer_backward(g_loc[0], saved_two, w_full[1], small_two, None)
        d_u, t_out_one, last, done_two, sm_one = layer_backward(d_hidden, saved_one, w_full[0], small_one, behind)
        t_z_one = dp_total(last[0])
        flat = []
        for one, two, i in zip(sm_one, sm_two, small_ids):
            for grad in (one, two):
                rounded = grad.astype(pieces[i].dtype) if pieces[i].dtype == BF16 else grad
                flat.append(rounded.astype(F32).reshape(-1))
        flat, t_z_one, s_x_one = lax.optimization_barrier((jnp.concatenate(flat), t_z_one, last[1]))
        t_x_one = dp_total(s_x_one)
        total = lax.psum(flat, ('dp', 'fsdp')) / batch_tot
        index = lax.axis_index('fsdp')
        small_out = []
        offset = 0
        for i, full in zip(small_ids, smalls):
            part = total[offset:offset + full.size].reshape(full.shape)
            offset += full.size
            width = pieces[i].shape[-1]
            small_out.append(lax.dynamic_slice_in_dim(part, index * width, width, axis=part.ndim - 1))
        g_in = jnp.zeros((pieces[1].shape[0], pieces[1].shape[2], pieces[1].shape[1]), F32)
        for layer, at_col, part in ((1, 0, done_two[0]), (1, d_inner, done_two[1]), (0, 0, t_z_one), (0, d_inner, t_x_one)):
            g_in = row_major(lax.dynamic_update_slice(g_in, part[None], (layer, at_col, 0)))
        g_in = jnp.swapaxes(g_in, 1, 2)
        g_w_out = jnp.zeros(pieces[8].shape, F32)
        for layer, part in ((1, t_out_two), (0, t_out_one)):
            g_w_out = lax.dynamic_update_slice(g_w_out, part[None], (layer, 0, 0))
        return (out_rows[None], d_u[None], small_out[0], g_in) + tuple(small_out[1:]) + (g_w_out,)

    return jax.shard_map(per_device, mesh=mesh, in_specs=(act_spec, act_spec) + weight_specs, out_specs=(act_spec, act_spec) + weight_specs, check_vma=False)
```

time: 5440 us -> 2530 us (0.47)
  waiting for transfers between devices: 2260 us -> 956 us
  other arithmetic: 1020 us -> 176 us
  local copies, waits for them, and re-layouts: 758 us -> 223 us
  matrix products: 1200 us -> 680 us
  Pallas kernels: 0 us -> 459 us
  blocking collectives: 173 us -> 0 us
    psum x2 -> x1, waiting for transfers between devices: 1680 us -> 32.4 us  [per_device(): total = lax.psum(flat, ('dp', 'fsdp')) / batch_tot]
    dot_general x42 -> x22, matrix products: 1200 us -> 680 us  [the longest x6 221 us: local_grad(): lax.dot_general(lhs, rhs, (((0,), (0,)), ((), ())), preferred_element_typ...]
    all_gather x4 -> x6, waiting for transfers between devices: 50.8 us -> 556 us  [gather(): return lax.all_gather(piece, 'fsdp', axis=0, tiled=True)]
    unnamed x16 -> x19, waiting for transfers between devices: 527 us -> 60.7 us
    pallas_call x0 -> x8, Pallas kernels: none -> 459 us  [the longest x2 229 us: ssd_backward(): pl.pallas_call(functools.partial(ssd_bwd_kernel, n_blk=n_blk), grid=(n_ch...]
    reduce_sum x17 -> x6, other arithmetic: 408 us -> 4.97 us  [the longest x2 4.11 us: dt_part(): dt_heads = jax.nn.softplus(dt_raw.astype(F32) + dt_bias)]
    reshape x27 -> x30, local copies, waits for them, and re-layouts: 359 us -> 15.2 us  [the longest x2 6.21 us: head_tables(): dt_heads.reshape(seq_len, n_heads // HEADS_BLK, HEADS_BLK)]
    ppermute x0 -> x6, waiting for transfers between devices: none -> 306 us  [dp_total(): moving = row_major(lax.ppermute(moving, 'dp', swap))]
  transfers between devices with their start and end apart: 12 -> 20, of which waited for: 4 -> 13; matrix products, arithmetic and copies ran while one was open for 32% -> 40% of each run, Pallas kernels for 0% -> 18%
where the time goes in v1:
time: 2530 us; the launch traced here: 2520 us
  waiting for transfers between devices  956 us (38%)
  matrix products  680 us (27%)
  Pallas kernels  459 us (18%)
  local copies, waits for them, and re-layouts  223 us (9%)
  other arithmetic  176 us (7%)
    all_gather x6, waiting for transfers between devices, gather(): return lax.all_gather(piece, 'fsdp', axis=0, tiled=True)  556 us
    ppermute x6, waiting for transfers between devices, dp_total(): moving = row_major(lax.ppermute(moving, 'dp', swap))  306 us
    pallas_call x2, Pallas kernels, ssd_backward(): pl.pallas_call(functools.partial(ssd_bwd_kernel, n_blk=n_blk), grid=(n_ch...  229 us
    dot_general x6, matrix products, local_grad(): lax.dot_general(lhs, rhs, (((0,), (0,)), ((), ())), preferred_element_typ...  221 us
    pallas_call x2, Pallas kernels, ssd_forward(): pl.pallas_call(ssd_fwd_kernel, grid=(n_chunks, n_blk), in_specs=[pl.Block...  112 us
    unnamed x173, local copies, waits for them, and re-layouts  81.2 us
    pallas_call x2, Pallas kernels, conv_backward(): pl.pallas_call(functools.partial(conv_bwd_kernel, n_cols=n_cols), grid=(n...  80.1 us
    dot_general x2, matrix products, layer_backward(): lax.dot_general(d_px, w_x, (((1,), (1,)), ((), ())), preferred_element_ty...  78.2 us
  transfers between devices with their start and end apart: 20, of which 13 were waited for; matrix products, arithmetic and copies ran while one was open for 40% of the time, Pallas kernels for 18%

profile of v1, /device:TPU:0, one launch (start us, length us, event | category | flops | bytes accessed | tf_op | source)
XLA Modules:
  0.0 2518.5 jit_solution(17769672771398953135)
XLA Ops:
  59.6 156.2 %all-gather.14.cloned.1.call-done = bf16[1,2560,5456]{1,2,0:T(8,128)(2,1)} async-done(((bf16[1,640,5456]{1,2,0:T(8,128)(2,1)}), bf16[1,2560,5456]{1,2,0:T(8,128)(2,1)}) %all-gather.14.cloned.1.call-update) | async-done | bytes 27934736 | tf_op jit(solution)/shard_map/all_gather | solution.py:429
  288.8 56.1 %ssd_forward.2 = (f32[1024,5120]{1,0:T(8,128)}, f32[4,128,5120]{2,1,0:T(8,128)}) custom-call(f32[1024,5376]{1,0:T(8,128)} %conv_forward.2.x_ref.b_ref.c_ref, f32[1024,5376]{1,0:T(8,128)} %conv_forward.2.x_ref.b_ref.c_ref, f32[1024,5376]{1,0:T(8,128)} %conv_forward.2.x_ref.b_ref.c_ref, f32[10,1024,8]{2,1,0:T(8,128)S(1)} %bitcast.194, ...), custom_call_target="tpu_custom_call" | custom-call | flops 60000002048 | bytes 50000000 | tf_op jit(solution)/shard_map/ssd_forward/pallas_call | solution.py:196
  375.8 38.4 %multiply_reduce_fusion.1 = (f32[1024]{0:T(1024)S(1)}, f32[1024,5120]{1,0:T(8,128)}, bf16[1024,5120]{1,0:T(8,128)(2,1)}) fusion(f32[1024,5120]{1,0:T(8,128)} %get-tuple-element.60.y_ref, bf16[1,2560,5120]{1,2,0:T(8,128)(2,1)} %all-gather.16.cloned.1.call-done, bf16[1,1024,2560]{2,1,0:T(8,128)(2,1)} %param.12, f32[2560]{0:T(1024)S(1)} %mul.343, ...), kind=kOutput, calls=%fused_computation.78 | convolution fusion | flops 26901217280 | bytes 83904512 | tf_op jit(solution)/shard_map/dot_general | solution.py:396
  414.2 121.7 %all-gather.18.cloned.1.call-done = bf16[1,5120,2560]{2,1,0:T(8,128)(2,1)} async-done(((bf16[1,1280,2560]{2,1,0:T(8,128)(2,1)}), bf16[1,5120,2560]{2,1,0:T(8,128)(2,1)}) %all-gather.18.cloned.1.call-update) | async-done | bytes 26214416 | tf_op jit(solution)/shard_map/all_gather | solution.py:429
  535.9 38.6 %fusion.66 = (f32[1024]{0:T(1024)S(1)}, bf16[1024,2560]{1,0:T(8,128)(2,1)}) fusion(bf16[1,5120,2560]{2,1,0:T(8,128)(2,1)} %all-gather.18.cloned.1.call-done, f32[1024,5120]{1,0:T(8,128)} %get-tuple-element.132, f32[5120]{0:T(1024)S(1)} %bitcast.242, f32[1024]{0:T(1024)S(1)} %fusion.130, bf16[1,1024,2560]{2,1,0:T(8,128)(2,1)} %param.12), kind=kOutput, calls=%fused_computation.107 | convolution fusion | flops 26875002880 | bytes 57700352 | tf_op jit(solution)/shard_map/dot_general | solution.py:398
  574.6 131.2 %all-gather.20.cloned.1.call-done = bf16[1,2560,5456]{1,2,0:T(8,128)(2,1)} async-done(((bf16[1,640,5456]{1,2,0:T(8,128)(2,1)}), bf16[1,2560,5456]{1,2,0:T(8,128)(2,1)}) %all-gather.20.cloned.1.call-update) | async-done | bytes 27934736 | tf_op jit(solution)/shard_map/all_gather | solution.py:429
  705.8 38.1 %fusion.53.p_ref = bf16[1024,5456]{1,0:T(8,128)(2,1)S(1)} fusion(bf16[1,2560,5456]{1,2,0:T(8,128)(2,1)} %all-gather.20.cloned.1.call-done, bf16[1024,2560]{1,0:T(8,128)(2,1)} %get-tuple-element.161, f32[2560]{0:T(1024)S(1)} %copy-done.31, f32[1024]{0:T(1024)S(1)} %fusion.131), kind=kOutput, calls=%fused_computation.96 | convolution fusion | flops 28621225984 | bytes 44365824 | tf_op jit(solution)/shard_map/dot_general | solution.py:390
  779.1 56.1 %ssd_forward.3 = (f32[1024,5120]{1,0:T(8,128)}, f32[4,128,5120]{2,1,0:T(8,128)}) custom-call(f32[1024,5376]{1,0:T(8,128)} %conv_forward.3.x_ref.b_ref.c_ref, f32[1024,5376]{1,0:T(8,128)} %conv_forward.3.x_ref.b_ref.c_ref, f32[1024,5376]{1,0:T(8,128)} %conv_forward.3.x_ref.b_ref.c_ref, f32[10,1024,8]{2,1,0:T(8,128)S(1)} %bitcast.198, ...), custom_call_target="tpu_custom_call" | custom-call | flops 60000002048 | bytes 50000000 | tf_op jit(solution)/shard_map/ssd_forward/pallas_call | solution.py:196
  865.6 38.8 %multiply_reduce_fusion = (f32[1024]{0:T(1024)S(1)}, f32[1024,5120]{1,0:T(8,128)}, bf16[1024,5120]{1,0:T(8,128)(2,1)}) fusion(f32[1024,5120]{1,0:T(8,128)} %get-tuple-element.62.y_ref, bf16[1,2560,5120]{1,2,0:T(8,128)(2,1)} %all-gather.22.cloned.1.call-done, bf16[1024,2560]{1,0:T(8,128)(2,1)} %get-tuple-element.161, f32[2560]{0:T(1024)S(1)} %copy-done.31, ...), kind=kOutput, calls=%fused_computation.71 | convolution fusion | flops 26901217280 | bytes 83904512 | tf_op jit(solution)/shard_map/dot_general | solution.py:396
  940.2 85.7 %all-gather.24.cloned.1.call-done = bf16[1,5120,2560]{2,1,0:T(8,128)(2,1)} async-done(((bf16[1,1280,2560]{2,1,0:T(8,128)(2,1)}), bf16[1,5120,2560]{2,1,0:T(8,128)(2,1)}) %all-gather.24.cloned.1.call-update) | async-done | bytes 26214416 | tf_op jit(solution)/shard_map/all_gather | solution.py:429
  1133.3 114.8 %ssd_backward.2 = (f32[1024,5376]{1,0:T(8,128)}, f32[1024,1280]{1,0:T(8,128)S(1)}, f32[1024,1280]{1,0:T(8,128)S(1)}, f32[4,8,5120]{2,1,0:T(8,128)S(1)}) custom-call(f32[1024,5120]{1,0:T(8,128)} %get-tuple-element.64.dy_ref, f32[1024,5120]{1,0:T(8,128)} %get-tuple-element.62.y_ref, f32[1024,5376]{1,0:T(8,128)} %conv_forward.3.x_ref.b_ref.c_ref, ...), custom_call_target="tpu_custom_call" | custom-call | flops 149999992832 | bytes 100000000 | tf_op jit(solution)/shard_map/ssd_backward/pallas_call | solution.py:237
  1269.9 40.1 %conv_backward.2 = (bf16[1024,5456]{1,0:T(8,128)(2,1)S(1)}, f32[8,5376]{1,0:T(8,128)S(1)}) custom-call(bf16[1024,5456]{1,0:T(8,128)(2,1)} %copy-done.12, f32[1024,5376]{1,0:T(8,128)} %get-tuple-element.68.d_ref, f32[4,5376]{1,0:T(4,128)S(1)} %copy-done.9, f32[1,5376]{1,0:T(1,128)S(1)} %copy-done.17, f32[1024,128]{1,0:T(8,128)S(1)} %pad.9.ddt_ref), custom_call_target="tpu_custom_call" | custom-call | flops 49999998976 | bytes 44000000 | tf_op jit(solution)/shard_map/conv_backward/pallas_call | solution.py:357
  1314.1 39.5 %multiply_convert_fusion.1 = bf16[2560,5456]{1,0:T(8,128)(2,1)} fusion(bf16[1024,5456]{1,0:T(8,128)(2,1)} %copy-done.21, bf16[1024,2560]{1,0:T(8,128)(2,1)} %get-tuple-element.161, f32[2560]{0:T(1024)S(1)} %copy-done.33, f32[1024]{0:T(1024)S(1)} %copy-done.41), kind=kOutput, calls=%fused_computation.1 | convolution fusion | flops 28643573760 | bytes 44365824 | tf_op jit(solution)/shard_map/dot_general | solution.py:438
  1355.1 38.1 %fusion = f32[1024,2560]{1,0:T(8,128)} fusion(bf16[1024,5456]{1,0:T(8,128)(2,1)} %copy-done.21, bf16[1,2560,5456]{1,2,0:T(8,128)(2,1)} %all-gather.20.cloned.1.call-done), kind=kOutput, calls=%fused_computation.14 | convolution fusion | flops 28605153280 | bytes 49594368 | tf_op jit(solution)/shard_map/dot_general | solution.py:494
  1436.2 60.8 %collective-permute-done = bf16[1280,2560]{1,0:T(8,128)(2,1)} collective-permute-done((bf16[1280,2560]{1,0:T(8,128)(2,1)}, bf16[1280,2560]{1,0:T(8,128)(2,1)}, u32[]{:S(2)}, u32[]{:S(2)}) %collective-permute-start) | collective-permute-done | bytes 6553632 | tf_op jit(solution)/shard_map/ppermute | solution.py:448
  1663.0 114.7 %ssd_backward.3 = (f32[1024,5376]{1,0:T(8,128)}, f32[1024,1280]{1,0:T(8,128)S(1)}, f32[1024,1280]{1,0:T(8,128)S(1)}, f32[4,8,5120]{2,1,0:T(8,128)S(1)}) custom-call(f32[1024,5120]{1,0:T(8,128)} %get-tuple-element.78.dy_ref, f32[1024,5120]{1,0:T(8,128)} %get-tuple-element.60.y_ref, f32[1024,5376]{1,0:T(8,128)} %conv_forward.2.x_ref.b_ref.c_ref, ...), custom_call_target="tpu_custom_call" | custom-call | flops 149999992832 | bytes 100000000 | tf_op jit(solution)/shard_map/ssd_backward/pallas_call | solution.py:237
  1826.4 40.1 %conv_backward.3 = (bf16[1024,5456]{1,0:T(8,128)(2,1)S(1)}, f32[8,5376]{1,0:T(8,128)S(1)}) custom-call(bf16[1024,5456]{1,0:T(8,128)(2,1)} %copy-done.10, f32[1024,5376]{1,0:T(8,128)} %get-tuple-element.84.d_ref, f32[4,5376]{1,0:T(4,128)S(1)} %copy-done.7, f32[1,5376]{1,0:T(1,128)S(1)} %copy-done.15, f32[1024,128]{1,0:T(8,128)S(1)} %pad.10.ddt_ref), custom_call_target="tpu_custom_call" | custom-call | flops 49999998976 | bytes 44000000 | tf_op jit(solution)/shard_map/conv_backward/pallas_call | solution.py:357
  1870.7 58.7 %reduce-scatter.23.cloned.1.call-done = bf16[640,5120]{1,0:T(8,128)(2,1)} async-done(((bf16[2560,5120]{1,0:T(8,128)(2,1)}), bf16[640,5120]{1,0:T(8,128)(2,1)}) %reduce-scatter.23.cloned.1.call-update) | async-done | bytes 6553616
  1938.9 39.1 %multiply_convert_fusion = bf16[2560,5456]{1,0:T(8,128)(2,1)} fusion(bf16[1024,5456]{1,0:T(8,128)(2,1)} %copy-done.20, bf16[1,1024,2560]{2,1,0:T(8,128)(2,1)} %param.12, f32[2560]{0:T(1024)S(1)} %copy-done.30, f32[1024]{0:T(1024)S(1)} %copy-done.38), kind=kOutput, calls=%fused_computation | convolution fusion | flops 28643573760 | bytes 44365824 | tf_op jit(solution)/shard_map/dot_general | solution.py:438
  1991.0 38.6 %fusion.94 = bf16[1,1024,2560]{2,1,0:T(8,128)(2,1)} fusion(bf16[1,5120,2560]{2,1,0:T(8,128)(2,1)} %all-gather.24.cloned.1.call-done, bf16[1024,2560]{1,0:T(8,128)(2,1)} %get-tuple-element.161, f32[1024,5120]{1,0:T(8,128)} %get-tuple-element.130, f32[5120]{0:T(1024)S(1)} %bitcast.241, f32[1024]{0:T(1024)S(1)} %copy-done.47), kind=kOutput, calls=%fused_computation.123 | convolution fusion | flops 26867138560 | bytes 57696256 | tf_op jit(solution)/shard_map/dot_general | solution.py:398
  2087.2 85.4 %collective-permute-done.3 = bf16[1280,2560]{1,0:T(8,128)(2,1)} collective-permute-done((bf16[1280,2560]{1,0:T(8,128)(2,1)}, bf16[1280,2560]{1,0:T(8,128)(2,1)}, u32[]{:S(2)}, u32[]{:S(2)}) %collective-permute-start.3) | collective-permute-done | bytes 6553632 | tf_op jit(solution)/shard_map/ppermute | solution.py:448
  2185.5 40.1 %fusion.65 = (bf16[2560]{0:T(1024)(128)(2,1)S(1)}, f32[1024]{0:T(1024)S(1)}, bf16[1024,2560]{1,0:T(8,128)(2,1)S(1)}) fusion(bf16[1,1024,2560]{2,1,0:T(8,128)(2,1)} %param.12, f32[1024]{0:T(1024)S(1)} %copy-done.38, f32[2560]{0:T(1024)S(1)} %copy-done.30, f32[1024,2560]{1,0:T(8,128)} %fusion.20, bf16[1024,5456]{1,0:T(8,128)(2,1)} %copy-done.20, ...), kind=kOutput, calls=%fused_computation.106 | convolution fusion | flops 28631363584 | bytes 60103680 | tf_op jit(solution)/shard_map/dot_general | solution.py:494
  2253.8 72.1 %collective-permute-done.4 = bf16[5120,640]{1,0:T(8,128)(2,1)} collective-permute-done((bf16[5120,640]{1,0:T(8,128)(2,1)}, bf16[5120,640]{1,0:T(8,128)(2,1)}, u32[]{:S(2)}, u32[]{:S(2)}) %collective-permute-start.4) | collective-permute-done | bytes 6553632 | tf_op jit(solution)/shard_map/ppermute | solution.py:448
  2416.8 83.4 %collective-permute-done.5 = bf16[5456,640]{1,0:T(8,128)(2,1)} collective-permute-done((bf16[5456,640]{1,0:T(8,128)(2,1)}, bf16[5456,640]{1,0:T(8,128)(2,1)}, u32[]{:S(2)}, u32[]{:S(2)}) %collective-permute-start.5) | collective-permute-done | bytes 6983712 | tf_op jit(solution)/shard_map/ppermute | solution.py:448
  (379 shorter events, 876.2 us)
Async XLA Ops:
  7.2 46.4 %all-reduce.9.cloned.1.call-start = ((), (), s32[]{:S(2)}) async-start(), calls=%async_computation.15 | async-start | bytes 557056
  16.1 199.8 %all-gather.14.cloned.1.call-start = ((), (), s32[]{:S(2)}) async-start(), calls=%async_computation.9 | async-start | bytes 34918400 | tf_op jit(solution)/shard_map/all_gather | solution.py:429
  26.3 349.5 %all-gather.16.cloned.1.call-start = ((), (), s32[]{:S(2)}) async-start(), calls=%async_computation.10 | async-start | bytes 32768000 | tf_op jit(solution)/shard_map/all_gather | solution.py:429
  37.0 498.9 %all-gather.18.cloned.1.call-start = ((), (), s32[]{:S(2)}) async-start(), calls=%async_computation.11 | async-start | bytes 32768000 | tf_op jit(solution)/shard_map/all_gather | solution.py:429
  47.4 658.4 %all-gather.20.cloned.1.call-start = ((), (), s32[]{:S(2)}) async-start(), calls=%async_computation.12 | async-start | bytes 34918400 | tf_op jit(solution)/shard_map/all_gather | solution.py:429
  48.0 817.6 %all-gather.22.cloned.1.call-start = ((), (), s32[]{:S(2)}) async-start(), calls=%async_computation.13 | async-start | bytes 32768000 | tf_op jit(solution)/shard_map/all_gather | solution.py:429
  48.6 977.3 %all-gather.24.cloned.1.call-start = ((), (), s32[]{:S(2)}) async-start(), calls=%async_computation.14 | async-start | bytes 32768000 | tf_op jit(solution)/shard_map/all_gather | solution.py:429
  49.3 1220.6 %reduce-scatter.15.cloned.1.call-start = ((), (), s32[]{:S(2)}) async-start(), calls=%async_computation.6 | async-start | bytes 32768000 | tf_op jit(solution)/shard_map/reduce_scatter | solution.py:442
  53.5 322.3 %copy-start.36 = (f32[1024]{0:T(1024)}, f32[1024]{0:T(1024)S(1)}, u32[]{:S(2)}) copy-start(f32[1024]{0:T(1024)S(1)} %fusion.129) | copy-start | bytes 12292
  57.5 318.3 %copy-start.28 = (f32[2560]{0:T(1024)}, f32[2560]{0:T(1024)S(1)}, u32[]{:S(2)}) copy-start(f32[2560]{0:T(1024)S(1)} %mul.343) | copy-start | bytes 30724
  58.9 697.5 %copy-start.16 = (f32[1,5376]{1,0:T(1,128)}, f32[1,5376]{1,0:T(1,128)S(1)}, u32[]{:S(2)}) copy-start(f32[1,5376]{1,0:T(1,128)S(1)} %slice.207.bias_ref) | copy-start | bytes 64516
  59.3 697.1 %copy-start.8 = (f32[4,5376]{1,0:T(4,128)}, f32[4,5376]{1,0:T(4,128)S(1)}, u32[]{:S(2)}) copy-start(f32[4,5376]{1,0:T(4,128)S(1)} %squeeze.44.w_ref) | copy-start | bytes 258052
  940.1 604.1 %reduce-scatter.19.cloned.1.call-start = ((), (), s32[]{:S(2)}) async-start(), calls=%async_computation.16 | async-start | bytes 32768000
  1132.7 682.0 %reduce-scatter.21.cloned.1.call-start = ((), (), s32[]{:S(2)}) async-start(), calls=%async_computation.17 | async-start | bytes 35225600
  1353.6 471.3 %reduce-scatter.17.cloned.1.call-start = ((), (), s32[]{:S(2)}) async-start(), calls=%async_computation.7 | async-start | bytes 32768000 | tf_op jit(solution)/shard_map/reduce_scatter | solution.py:442
  1353.6 143.3 %collective-permute-start = (bf16[1280,2560]{1,0:T(8,128)(2,1)}, bf16[1280,2560]{1,0:T(8,128)(2,1)}, u32[]{:S(2)}, u32[]{:S(2)}) collective-permute-start(bf16[1280,2560]{1,0:T(8,128)(2,1)} %reduce-scatter.15.cloned.1.call-done), channel_id=1, source_target_pairs={{0,4},{4,0},{1,5},{5,1},{2,6},{6,2},{3,7},{7,3}} | collective-permute-start | bytes 19660808 | tf_op jit(solution)/shard_map/ppermute | solution.py:448
  1544.1 385.3 %reduce-scatter.23.cloned.1.call-start = ((), (), s32[]{:S(2)}) async-start(), calls=%async_computation.18 | async-start | bytes 32768000
  1661.5 675.1 %reduce-scatter.25.cloned.1.call-start = ((), (), s32[]{:S(2)}) async-start(), calls=%async_computation.19 | async-start | bytes 35225600
  1661.5 142.6 %collective-permute-start.1 = (bf16[5120,640]{1,0:T(8,128)(2,1)}, bf16[5120,640]{1,0:T(8,128)(2,1)}, u32[]{:S(2)}, u32[]{:S(2)}) collective-permute-start(bf16[5120,640]{1,0:T(8,128)(2,1)} %bitcast.215), channel_id=1, source_target_pairs={{0,4},{4,0},{1,5},{5,1},{2,6},{6,2},{3,7},{7,3}} | collective-permute-start | bytes 19660808 | tf_op jit(solution)/shard_map/ppermute | solution.py:448
  1824.9 153.1 %collective-permute-start.2 = (bf16[5456,640]{1,0:T(8,128)(2,1)}, bf16[5456,640]{1,0:T(8,128)(2,1)}, u32[]{:S(2)}, u32[]{:S(2)}) collective-permute-start(bf16[5456,640]{1,0:T(8,128)(2,1)} %bitcast.211), channel_id=1, source_target_pairs={{0,4},{4,0},{1,5},{5,1},{2,6},{6,2},{3,7},{7,3}} | collective-permute-start | bytes 20951048 | tf_op jit(solution)/shard_map/ppermute | solution.py:448
  1989.6 421.1 %all-reduce.7.cloned.1.call-start = ((), (), s32[]{:S(2)}) async-start(), calls=%async_computation.8 | async-start | bytes 557056 | tf_op jit(solution)/shard_map/psum | solution.py:519
  2030.0 142.6 %collective-permute-start.3 = (bf16[1280,2560]{1,0:T(8,128)(2,1)}, bf16[1280,2560]{1,0:T(8,128)(2,1)}, u32[]{:S(2)}, u32[]{:S(2)}) collective-permute-start(bf16[1280,2560]{1,0:T(8,128)(2,1)} %reduce-scatter.17.cloned.1.call-done), channel_id=1, source_target_pairs={{0,4},{4,0},{1,5},{5,1},{2,6},{6,2},{3,7},{7,3}} | collective-permute-start | bytes 19660808 | tf_op jit(solution)/shard_map/ppermute | solution.py:448
  2184.0 141.9 %collective-permute-start.4 = (bf16[5120,640]{1,0:T(8,128)(2,1)}, bf16[5120,640]{1,0:T(8,128)(2,1)}, u32[]{:S(2)}, u32[]{:S(2)}) collective-permute-start(bf16[5120,640]{1,0:T(8,128)(2,1)} %bitcast.213), channel_id=1, source_target_pairs={{0,4},{4,0},{1,5},{5,1},{2,6},{6,2},{3,7},{7,3}} | collective-permute-start | bytes 19660808 | tf_op jit(solution)/shard_map/ppermute | solution.py:448
  2346.6 153.7 %collective-permute-start.5 = (bf16[5456,640]{1,0:T(8,128)(2,1)}, bf16[5456,640]{1,0:T(8,128)(2,1)}, u32[]{:S(2)}, u32[]{:S(2)}) collective-permute-start(bf16[5456,640]{1,0:T(8,128)(2,1)} %bitcast.209), channel_id=1, source_target_pairs={{0,4},{4,0},{1,5},{5,1},{2,6},{6,2},{3,7},{7,3}} | collective-permute-start | bytes 20951048 | tf_op jit(solution)/shard_map/ppermute | solution.py:448
  (79 other events, 3807.9 us)
Sparse Core Ops, SparseCore 0:
  16.2 29.3 all-reduce.8
  47.6 168.1 all-gather.13
  217.4 158.3 all-gather.15
  377.2 158.6 all-gather.17
  537.8 167.8 all-gather.19
  707.2 158.3 all-gather.21
  867.2 158.6 all-gather.23
  1029.0 175.3 reduce-scatter.14
  1207.5 175.3 reduce-scatter.18
  1386.0 187.0 reduce-scatter.20
  1575.6 175.3 reduce-scatter.16
  1754.0 175.3 reduce-scatter.22
  1989.7 187.0 reduce-scatter.24
  2367.9 42.7 all-reduce.6
